TPU v7x, 128 devices: a whole 4x4x4 slice. The times are simulated.
128 devices in a mesh: seq: 16 (over z, y_lo, core), head: 8 (over x, y_hi).
Axes of the slice: x: 4, y: 4 (y_hi: 2, y_lo: 2; y = y_hi * 2 + y_lo), z: 4, core: 2. Of those that a mesh axis runs over, the one named last changes fastest.
Arguments:
- tokens: bfloat16 [128, 512, 1024], P('seq'), may hold values from -36 to 36
- lengths: int32 [128], P('seq'), may hold values from 1 to 512, 32768 in all
- attn_in: float32 [1024, 3, 1024], P(('seq', 'head')), may hold values from -0.4 to 0.4
- attn_out: float32 [1024, 1024], P(None, ('seq', 'head')), may hold values from -0.1875 to 0.1875
- mlp_in: float32 [1024, 4096], P(('seq', 'head')), may hold values from -0.1875 to 0.1875
- mlp_out: float32 [4096, 1024], P(None, ('seq', 'head')), may hold values from -0.09375 to 0.09375
- norm_gain: float32 [2, 1024], replicated, may hold values from 0.5 to 1.5
- norm_shift: float32 [2, 1024], replicated, may hold values from -3 to 3
Outputs:
- encoded: bfloat16 [128, 512, 1024], P('seq', 'head')
- key_cache: bfloat16 [128, 512, 1024], P('seq', None, 'head')
- value_cache: bfloat16 [128, 512, 1024], P('seq', None, 'head')
Inputs may be any that keep to these rules, and one draw needn't show every extreme that they name: `lengths`: some prompt has exactly 512 tokens.
All inputs are finite; a program needn't handle non-finite values. No bound on the sum of `lengths` on one device may be relied on, other than what follows from the above.
Results may differ from a plain program's by a relative error of at most 0.02.
Values may be sent and summed in bfloat16 or wider, within the bound.
A program may use at most 128 MiB of HBM per device.

v0:
```python
import math
import jax
import jax.numpy as jnp
from jax import lax
from jax.sharding import PartitionSpec as P

DH = 64
EPSILON = 1e-05
CHUNKS = 1


def layer_norm(values, gain, shift):
    center = values - jnp.mean(values, axis=-1, keepdims=True)
    spread = jnp.mean(center * center, axis=-1, keepdims=True)
    return center * lax.rsqrt(spread + EPSILON) * gain + shift


def regroup_weights(attn_in, attn_out, mlp_in, mlp_out, heads_axis, seq_axis):
    rows = attn_in.shape[0]
    model_width = attn_in.shape[2]
    hidden_width = mlp_in.shape[1]
    block_width = model_width // heads_axis
    in_piece = attn_in.astype(jnp.bfloat16).reshape(rows, 3, heads_axis, block_width)
    in_piece = jnp.transpose(in_piece, (0, 2, 1, 3)).reshape(rows, heads_axis, 3 * block_width)
    whole_rows = jnp.concatenate(
        [
            attn_out.astype(jnp.bfloat16).T,
            mlp_in.astype(jnp.bfloat16),
            mlp_out.astype(jnp.bfloat16).T,
        ],
        axis=1,
    )
    whole_piece = jnp.broadcast_to(whole_rows[:, None], (rows, heads_axis, whole_rows.shape[1]))
    packed = jnp.concatenate([in_piece, whole_piece], axis=2)
    packed = lax.all_to_all(packed, "head", 1, 0, tiled=True)
    packed = packed.reshape(rows * heads_axis, packed.shape[2])
    in_part = packed[:, : 3 * block_width]
    in_part = jnp.broadcast_to(in_part[None], (seq_axis,) + in_part.shape)
    qkv_weight = lax.all_to_all(in_part, "seq", 0, 0, tiled=True)
    qkv_weight = qkv_weight.reshape(-1, 3, block_width)
    early_end = 3 * block_width + model_width + hidden_width
    early = lax.all_gather(packed[:, 3 * block_width : early_end], "seq", axis=0, tiled=True)
    proj_weight_t = early[:, :model_width]
    up_weight = early[:, model_width:]
    down_weight_t = lax.all_gather(packed[:, early_end:], "seq", axis=0, tiled=True)
    return (qkv_weight, proj_weight_t, up_weight, down_weight_t)


def encode_chunk(
    tokens,
    lengths,
    qkv_weight,
    proj_weight_t,
    up_weight,
    down_weight_t,
    norm_gain,
    norm_shift,
    heads_axis,
    head_index,
):
    prompts = tokens.shape[0]
    seq_len = tokens.shape[1]
    model_width = tokens.shape[2]
    hidden_width = up_weight.shape[1]
    block_width = model_width // heads_axis
    hidden_block = hidden_width // heads_axis
    local_heads = block_width // DH
    row_count = seq_len // heads_axis
    row_start = head_index * row_count
    projected = jnp.einsum(
        "pld,dte->plte", tokens, qkv_weight, preferred_element_type=jnp.float32
    ).astype(jnp.bfloat16)
    positions = jnp.arange(seq_len, dtype=jnp.int32)
    inside = positions[None, :] < lengths[:, None]
    key_part = projected[:, :, 1]
    value_part = projected[:, :, 2]
    queries = projected[:, :, 0].reshape(prompts, seq_len, local_heads, DH)
    key_heads = key_part.reshape(prompts, seq_len, local_heads, DH)
    value_heads = value_part.reshape(prompts, seq_len, local_heads, DH)
    scores = jnp.einsum(
        "pqhd,pkhd->phqk", queries, key_heads, preferred_element_type=jnp.float32
    ) * (1.0 / math.sqrt(DH))
    scores = jnp.where(inside[:, None, None, :], scores, -1e30)
    row_peak = jnp.max(scores, axis=-1, keepdims=True)
    raised = jnp.exp(scores - row_peak)
    weights = (raised / jnp.sum(raised, axis=-1, keepdims=True)).astype(jnp.bfloat16)
    context = jnp.einsum(
        "phqk,pkhd->pqhd", weights, value_heads, preferred_element_type=jnp.float32
    )
    context = context.astype(jnp.bfloat16).reshape(prompts, heads_axis, row_count, block_width)
    key_cache = jnp.where(inside[:, :, None], key_part, jnp.zeros_like(key_part))
    value_cache = jnp.where(inside[:, :, None], value_part, jnp.zeros_like(value_part))
    context_blocks = jnp.transpose(context, (1, 0, 2, 3))
    context_blocks = lax.all_to_all(context_blocks, "head", 0, 0, tiled=True)
    proj_blocks = proj_weight_t.reshape(model_width, heads_axis, block_width)
    attn_rows = jnp.einsum(
        "sprf,esf->pre", context_blocks, proj_blocks, preferred_element_type=jnp.float32
    )
    token_rows = lax.dynamic_slice_in_dim(tokens, row_start, row_count, 1)
    normed_rows = layer_norm(
        token_rows.astype(jnp.float32) + attn_rows, norm_gain[0], norm_shift[0]
    ).astype(jnp.bfloat16)
    hidden = jax.nn.gelu(
        jnp.einsum("pld,df->plf", normed_rows, up_weight, preferred_element_type=jnp.float32),
        approximate=False,
    ).astype(jnp.bfloat16)
    hidden = lax.optimization_barrier(hidden)
    mlp_rows = jnp.einsum("plf,ef->ple", hidden, down_weight_t, preferred_element_type=jnp.float32)
    finished = layer_norm(normed_rows.astype(jnp.float32) + mlp_rows, norm_gain[1], norm_shift[1])
    inside_rows = lax.dynamic_slice_in_dim(inside, row_start, row_count, 1)
    encoded = jnp.where(inside_rows[:, :, None], finished, 0.0).astype(jnp.bfloat16)
    return (encoded, key_cache, value_cache)


def shards(tokens, lengths, attn_in, attn_out, mlp_in, mlp_out, norm_gain, norm_shift):
    heads_axis = lax.axis_size("head")
    head_index = lax.axis_index("head")
    qkv_weight, proj_weight_t, up_weight, down_weight_t = regroup_weights(
        attn_in, attn_out, mlp_in, mlp_out, heads_axis, lax.axis_size("seq")
    )
    prompts = tokens.shape[0]
    chunk = max(1, prompts // CHUNKS)
    pieces = []
    for lower in range(0, prompts, chunk):
        pieces.append(
            encode_chunk(
                tokens[lower : lower + chunk],
                lengths[lower : lower + chunk],
                qkv_weight,
                proj_weight_t,
                up_weight,
                down_weight_t,
                norm_gain,
                norm_shift,
                heads_axis,
                head_index,
            )
        )
    return tuple((jnp.concatenate(parts, axis=0) for parts in zip(*pieces)))


def solution(mesh):
    in_specs = (
        P("seq", None, None),
        P("seq"),
        P(("seq", "head"), None, None),
        P(None, ("seq", "head")),
        P(("seq", "head"), None),
        P(None, ("seq", "head")),
        P(),
        P(),
    )
    out_specs = (P("seq", "head", None), P("seq", None, "head"), P("seq", None, "head"))
    return jax.shard_map(shards, mesh=mesh, in_specs=in_specs, out_specs=out_specs, check_vma=False)
```

profile of v0, /device:TPU:25, one launch (start us, length us, event | category | flops | bytes accessed | tf_op | source)
XLA Modules:
  0.0 181.5 jit_solution(4619803239640551789)
XLA Ops:
  7.2 0.0 copy-start.3
  7.2 0.0 all-gather.3.cloned.1.call-start
  7.2 0.9 convert_bitcast_fusion.1
  8.1 0.9 convert_element_type.45
  9.0 0.8 convert_bitcast_fusion.3
  9.8 0.9 copy_bitcast_fusion
  10.7 0.1 broadcast_in_dim.36
  10.8 0.1 pad_maximum_fusion
  10.9 22.5 %all_to_all.25 = bf16[8,8,9600]{2,0,1:T(8,128)(2,1)S(1)} all-to-all(bf16[8,8,9600]{2,0,1:T(8,128)(2,1)S(1)} %pad_maximum_fusion), channel_id=1, replica_groups=mesh['seq'=16,'head'=8] {'head'}, dimensions={1} | all-to-all | bytes 2457600 | tf_op jit(solution)/shard_map/all_to_all | solution.py:35
  33.4 0.9 slice.52
  34.3 0.0 all-gather.3.cloned.1.call-update
  34.3 0.0 all-gather.5.cloned.1.call-start
  34.3 0.8 slice.55
  35.2 0.0 all-gather.5.cloned.1.call-update
  35.2 1.0 broadcast_in_dim.37
  36.2 8.3 %all-to-all-start.1 = ((bf16[16,64,384]{2,1,0:T(8,128)(2,1)}), bf16[16,64,384]{2,1,0:T(8,128)(2,1)S(1)}, u32[]{:S(2)}, u32[]{:S(2)}) async-start(bf16[16,64,384]{2,1,0:T(8,128)(2,1)} %broadcast_in_dim.37), calls=%async_computation.1 | async-start | bytes 1572864 | tf_op jit(solution)/shard_map/all_to_all | solution.py:39
  44.5 0.0 copy-done.3
  44.5 0.1 iota_compare_fusion
  44.5 17.6 %all-to-all-done.1 = bf16[16,64,384]{2,1,0:T(8,128)(2,1)S(1)} async-done(((bf16[16,64,384]{2,1,0:T(8,128)(2,1)}), bf16[16,64,384]{2,1,0:T(8,128)(2,1)S(1)}, u32[]{:S(2)}, u32[]{:S(2)}) %all-to-all-start.1) | async-done | bytes 786464 | tf_op jit(solution)/shard_map/all_to_all | solution.py:39
  62.1 1.1 reshape.96
  63.2 7.4 %convert_bitcast_fusion = bf16[8,512,3,128]{1,3,0,2:T(8,128)(2,1)S(1)} fusion(bf16[8,512,1024]{2,1,0:T(8,128)(2,1)} %param.8, bf16[1024,3,128,1]{2,1,0,3:T(4,128)(2,1)} %bitcast.74), kind=kOutput, calls=%fused_computation.34 | convolution fusion | flops 3222798336 | bytes 12320768 | tf_op jit(solution)/shard_map/pld,dte->plte/dot_general | solution.py:70
  70.6 1.8 fusion.32
  72.3 10.8 %fusion.35 = (f32[8,2,512]{2,1,0:T(2,128)S(1)}, f32[8,2,512,512]{2,3,1,0:T(8,128)}) fusion(pred[8,512]{1,0:T(8,128)(4,1)S(1)} %iota_compare_fusion, bf16[8,512,2,64]{1,3,2,0:T(8,128)(2,1)} %bitcast.77, bf16[8,512,2,64]{1,3,2,0:T(8,128)(2,1)} %bitcast.76), kind=kOutput, calls=%fused_computation.64 | convolution fusion | flops 553648640 | bytes 18911232 | tf_op jit(solution)/shard_map/sub | solution.py:85
  83.1 9.0 %fusion.28 = bf16[8,512,2,64]{1,3,2,0:T(8,128)(2,1)} fusion(bf16[8,512,2,64]{1,3,2,0:T(8,128)(2,1)} %bitcast.75, f32[8,2,512,512]{2,3,1,0:T(8,128)} %get-tuple-element.22, f32[8,2,512]{2,1,0:T(2,128)S(1)} %get-tuple-element.21), kind=kOutput, calls=%fused_computation.43 | convolution fusion | flops 545783808 | bytes 18907136 | tf_op jit(solution)/shard_map/phqk,pkhd->pqhd/dot_general | solution.py:87
  92.2 0.0 copy-start.1
  92.2 0.0 copy-start.2
  92.2 3.9 %reshape.97 = bf16[8,8,64,128]{2,1,3,0:T(8,128)(2,1)} reshape(bf16[8,512,2,64]{1,3,2,0:T(8,128)(2,1)} %fusion.28) | data formatting | bytes 2097152 | tf_op jit(solution)/shard_map/reshape | solution.py:90
  96.1 3.4 %copy.28 = bf16[8,8,64,128]{3,2,1,0:T(8,128)(2,1)} copy(bf16[8,8,64,128]{2,0,3,1:T(8,128)(2,1)} %bitcast.69) | data formatting | bytes 2097152 | tf_op jit(solution)/shard_map/transpose | solution.py:93
  99.4 6.6 %all-to-all-start.2 = ((bf16[8,8,64,128]{3,2,1,0:T(8,128)(2,1)}), bf16[8,8,64,128]{3,2,1,0:T(8,128)(2,1)}, u32[]{:S(2)}, u32[]{:S(2)}) async-start(bf16[8,8,64,128]{3,2,1,0:T(8,128)(2,1)} %copy.28), calls=%async_computation.2 | async-start | bytes 2097152 | tf_op jit(solution)/shard_map/all_to_all | solution.py:94
  106.0 0.1 constant_dynamic-slice_fusion
  106.1 0.0 copy-done.1
  106.1 0.0 copy-done.2
  106.1 1.5 bitcast_select_fusion
  107.6 2.3 %copy.32 = bf16[8,512,128]{2,1,0:T(8,128)(2,1)} copy(bf16[8,512,128]{1,2,0:T(8,128)(2,1)} %get-tuple-element.13) | data formatting | bytes 2097152
  109.8 2.3 %copy.33 = bf16[8,512,128]{2,1,0:T(8,128)(2,1)} copy(bf16[8,512,128]{1,2,0:T(8,128)(2,1)} %get-tuple-element.12) | data formatting | bytes 2097152
  112.1 0.0 all-gather.3.cloned.1.call-done
  112.1 1.8 slice.53
  113.9 2.6 %copy.29 = bf16[1024,1024]{0,1:T(8,128)(2,1)} copy(bf16[1024,1024]{1,0:T(8,128)(2,1)S(1)} %slice.53) | data formatting | bytes 4194304 | tf_op jit(solution)/shard_map/slice | solution.py:43
  116.4 5.1 %all-to-all-done.2 = bf16[8,8,64,128]{3,2,1,0:T(8,128)(2,1)} async-done(((bf16[8,8,64,128]{3,2,1,0:T(8,128)(2,1)}), bf16[8,8,64,128]{3,2,1,0:T(8,128)(2,1)}, u32[]{:S(2)}, u32[]{:S(2)}) %all-to-all-start.2) | async-done | bytes 1048608 | tf_op jit(solution)/shard_map/all_to_all | solution.py:94
  121.5 0.0 copy-start
  121.5 3.7 %fusion.36 = (f32[8,64]{1,0:T(8,128)S(1)}, f32[8,64,1024]{2,1,0:T(8,128)S(1)}) fusion(bf16[8,8,64,128]{3,2,1,0:T(8,128)(2,1)} %all-to-all-done.2, bf16[1024,8,128,1]{0,2,3,1:T(8,128)(2,1)} %bitcast.73, bf16[8,512,1024]{2,1,0:T(8,128)(2,1)} %param.8, s32[]{:T(128)S(6)} %select_n.19), kind=kOutput, calls=%fused_computation.65 | convolution fusion | flops 1075314176 | bytes 6293508 | tf_op jit(solution)/shard_map/sprf,esf->pre/dot_general | solution.py:96
  125.2 0.3 multiply_reduce_fusion.1
  125.6 1.4 copy-done
  127.0 23.4 %fusion.4 = bf16[8,64,4096]{2,1,0:T(8,128)(2,1)} fusion(bf16[1024,5120]{1,0:T(8,128)(2,1)S(1)} %copy-done, f32[8,64,1024]{2,1,0:T(8,128)S(1)} %get-tuple-element.24, f32[1024]{0:T(1024)S(1)} %bitcast.82, f32[1024]{0:T(1024)S(1)} %bitcast.80, f32[8,64]{1,0:T(8,128)S(1)} %add_rsqrt_fusion.1, f32[8,64]{1,0:T(8,128)S(1)} %broadcast_multiply_fusion.1), kind=kOutput, calls=%fused_computation.8 | convolution fusion | flops 4433903616 | bytes 14696448 | tf_op jit(solution)/shard_map/pld,df->plf/dot_general | solution.py:104
  150.4 12.9 %all-gather.5.cloned.1.call-done = bf16[1024,4096]{1,0:T(8,128)(2,1)} async-done(((bf16[64,4096]{1,0:T(8,128)(2,1)}), bf16[1024,4096]{1,0:T(8,128)(2,1)}) %all-gather.5.cloned.1.call-update) | async-done | bytes 8388624 | tf_op jit(solution)/shard_map/all_gather | solution.py:45
  163.3 8.4 %fusion.37 = (f32[8,64]{1,0:T(8,128)S(1)}, f32[8,64,1024]{2,1,0:T(8,128)S(1)}) fusion(bf16[8,64,4096]{2,1,0:T(8,128)(2,1)} %fusion.4, bf16[1024,4096]{1,0:T(8,128)(2,1)} %all-gather.5.cloned.1.call-done, f32[1024]{0:T(1024)S(1)} %bitcast.83, f32[1024]{0:T(1024)S(1)} %bitcast.81, f32[8,64]{1,0:T(8,128)S(1)} %add_rsqrt_fusion.1, ...), kind=kOutput, calls=%fused_computation.66 | convolution fusion | flops 4299161088 | bytes 16791552 | tf_op jit(solution)/shard_map/plf,ef->ple/dot_general | solution.py:108
  171.7 0.3 multiply_reduce_fusion
  172.1 2.6 %select_convert_fusion = bf16[8,64,1024]{2,1,0:T(8,128)(2,1)} fusion(f32[8,64,1024]{2,1,0:T(8,128)S(1)} %get-tuple-element.26, f32[1024]{0:T(1024)S(1)} %bitcast.79, f32[1024]{0:T(1024)S(1)} %bitcast.78, f32[8,64]{1,0:T(8,128)S(1)} %add_rsqrt_fusion, f32[8,64]{1,0:T(8,128)S(1)} %broadcast_multiply_fusion, pred[8,64]{1,0:T(8,128)(4,1)S(1)} %constant_dynamic-slice_fusion), kind=kLoop, calls=%fused_computation.36 | loop fusion | flops 3145728 | bytes 3158528 | tf_op jit(solution)/shard_map/convert_element_type | solution.py:111
  (8 shorter events, 0.1 us)
Async XLA Ops:
  7.2 37.3 %copy-start.3 = (s32[8]{0:T(128)S(1)}, s32[8]{0:T(128)}, u32[]{:S(2)}) copy-start(s32[8]{0:T(128)} %param.9) | copy-start | bytes 100
  7.2 104.9 %all-gather.3.cloned.1.call-start = ((), (), s32[]{:S(2)}) async-start(), calls=%async_computation.3 | async-start | bytes 11141120 | tf_op jit(solution)/shard_map/all_gather | solution.py:42
  34.3 129.0 %all-gather.5.cloned.1.call-start = ((), (), s32[]{:S(2)}) async-start(), calls=%async_computation.4 | async-start | bytes 8912896 | tf_op jit(solution)/shard_map/all_gather | solution.py:45
  36.2 25.9 %all-to-all-start.1 = ((bf16[16,64,384]{2,1,0:T(8,128)(2,1)}), bf16[16,64,384]{2,1,0:T(8,128)(2,1)S(1)}, u32[]{:S(2)}, u32[]{:S(2)}) async-start(bf16[16,64,384]{2,1,0:T(8,128)(2,1)} %broadcast_in_dim.37), calls=%async_computation.1 | async-start | bytes 1572864 | tf_op jit(solution)/shard_map/all_to_all | solution.py:39
  92.2 13.9 %copy-start.1 = (f32[2,1024]{1,0:T(2,128)S(1)}, f32[2,1024]{1,0:T(2,128)}, u32[]{:S(2)}) copy-start(f32[2,1024]{1,0:T(2,128)} %param.14) | copy-start | bytes 24580
  92.2 13.9 %copy-start.2 = (f32[2,1024]{1,0:T(2,128)S(1)}, f32[2,1024]{1,0:T(2,128)}, u32[]{:S(2)}) copy-start(f32[2,1024]{1,0:T(2,128)} %param.15) | copy-start | bytes 24580
  99.4 22.1 %all-to-all-start.2 = ((bf16[8,8,64,128]{3,2,1,0:T(8,128)(2,1)}), bf16[8,8,64,128]{3,2,1,0:T(8,128)(2,1)}, u32[]{:S(2)}, u32[]{:S(2)}) async-start(bf16[8,8,64,128]{3,2,1,0:T(8,128)(2,1)} %copy.28), calls=%async_computation.2 | async-start | bytes 2097152 | tf_op jit(solution)/shard_map/all_to_all | solution.py:94
  121.5 5.4 %copy-start = (bf16[1024,5120]{1,0:T(8,128)(2,1)S(1)}, bf16[1024,5120]{1,0:T(8,128)(2,1)}, u32[]{:S(2)}) copy-start(bf16[1024,5120]{1,0:T(8,128)(2,1)} %all-gather.3.cloned.1.call-done) | copy-start | bytes 31457284
Sparse Core Ops, SparseCore 0:
  34.4 72.0 all-gather.2
  108.2 55.0 all-gather.4
where the time goes:
time: 182 us; the launch traced here: 181 us
  matrix products  62.7 us (34%)
  waiting for transfers between devices  35.6 us (20%)
  local copies, waits for them, and re-layouts  23.2 us (13%)
  blocking collectives  22.5 us (12%)
  starting transfers between devices  14.9 us (8%)
  between operations  14.2 us (8%)
  other arithmetic  8.38 us (5%)
    dot_general x1, matrix products, encode_chunk(): jnp.einsum('pld,df->plf', normed_rows, up_weight, preferred_element_type=...  23.4 us
    all_to_all x1, blocking collectives, regroup_weights(): packed = lax.all_to_all(packed, 'head', 1, 0, tiled=True)  22.5 us
    all_to_all x1, waiting for transfers between devices, regroup_weights(): qkv_weight = lax.all_to_all(in_part, 'seq', 0, 0, tiled=True)  17.6 us
    all_gather x1, waiting for transfers between devices, regroup_weights(): lax.all_gather(packed[:, early_end:], 'seq', axis=0, tiled=True)  12.9 us
    sub x1, matrix products, encode_chunk(): raised = jnp.exp(scores - row_peak)  10.8 us
    dot_general x1, matrix products, encode_chunk(): jnp.einsum('phqk,pkhd->pqhd', weights, value_heads, preferred_element_typ...  9 us
    dot_general x1, matrix products, encode_chunk(): jnp.einsum('plf,ef->ple', hidden, down_weight_t, preferred_element_type=j...  8.42 us
    all_to_all x1, starting transfers between devices, regroup_weights(): qkv_weight = lax.all_to_all(in_part, 'seq', 0, 0, tiled=True)  8.29 us
  transfers between devices with their start and end apart: 4, of which 3 were waited for; matrix products, arithmetic and copies ran while one was open for 42% of the time, Pallas kernels for 0%

commit v1 on v0

--- a/solution.py
+++ b/solution.py
@@ -42,7 +42,11 @@
     early = lax.all_gather(packed[:, 3 * block_width : early_end], "seq", axis=0, tiled=True)
     proj_weight_t = early[:, :model_width]
     up_weight = early[:, model_width:]
-    down_weight_t = lax.all_gather(packed[:, early_end:], "seq", axis=0, tiled=True)
+    own = packed[:, early_end:]
+    count = lax.axis_size("seq")
+    cells = jnp.stack([own for _ in range(count)])
+    cells = lax.all_to_all(cells, "seq", split_axis=0, concat_axis=0)
+    down_weight_t = jnp.concatenate(cells, axis=0)
     return (qkv_weight, proj_weight_t, up_weight, down_weight_t)
 
 

time: 182 us -> 248 us (1.36)
  waiting for transfers between devices: 35.6 us -> 84.9 us
  starting transfers between devices: 14.9 us -> 23.6 us
  local copies, waits for them, and re-layouts: 23.2 us -> 29.5 us
    all_to_all x0 -> x1, waiting for transfers between devices: none -> 55.1 us  [regroup_weights(): cells = lax.all_to_all(cells, 'seq', split_axis=0, concat_axis=0)]
    all_gather x1 -> x0, waiting for transfers between devices: 12.9 us -> none  [regroup_weights(): lax.all_gather(packed[:, early_end:], 'seq', axis=0, tiled=True)]
    all_to_all x1, waiting for transfers between devices: 5.11 us -> 13.3 us  [encode_chunk(): context_blocks = lax.all_to_all(context_blocks, 'head', 0, 0, tiled=True)]
    all_to_all x0 -> x1, starting transfers between devices: none -> 7.42 us  [regroup_weights(): cells = lax.all_to_all(cells, 'seq', split_axis=0, concat_axis=0)]
    another operation x0 -> x1, local copies, waits for them, and re-layouts: none -> 5.34 us  [regroup_weights(): cells = jnp.stack([own for _ in range(count)])]
    unnamed x10 -> x12, local copies, waits for them, and re-layouts: 5.91 us -> 5.74 us
  transfers between devices with their start and end apart: 4 -> 4, of which waited for: 3 -> 3; matrix products, arithmetic and copies ran while one was open for 42% -> 34% of each run, Pallas kernels for 0% -> 0%
where the time goes in v1:
time: 248 us; the launch traced here: 246 us
  waiting for transfers between devices  84.9 us (34%)
  matrix products  62.6 us (25%)
  local copies, waits for them, and re-layouts  29.5 us (12%)
  starting transfers between devices  23.6 us (10%)
  blocking collectives  22.5 us (9%)
  between operations  14.2 us (6%)
  other arithmetic  8.38 us (3%)
    all_to_all x1, waiting for transfers between devices, regroup_weights(): cells = lax.all_to_all(cells, 'seq', split_axis=0, concat_axis=0)  55.1 us
    dot_general x1, matrix products, encode_chunk(): jnp.einsum('pld,df->plf', normed_rows, up_weight, preferred_element_type=...  23.4 us
    all_to_all x1, blocking collectives, regroup_weights(): packed = lax.all_to_all(packed, 'head', 1, 0, tiled=True)  22.5 us
    all_to_all x1, waiting for transfers between devices, regroup_weights(): qkv_weight = lax.all_to_all(in_part, 'seq', 0, 0, tiled=True)  16.5 us
    all_to_all x1, waiting for transfers between devices, encode_chunk(): context_blocks = lax.all_to_all(context_blocks, 'head', 0, 0, tiled=True)  13.3 us
    sub x1, matrix products, encode_chunk(): raised = jnp.exp(scores - row_peak)  10.8 us
    dot_general x1, matrix products, encode_chunk(): jnp.einsum('phqk,pkhd->pqhd', weights, value_heads, preferred_element_typ...  8.99 us
    dot_general x1, matrix products, encode_chunk(): jnp.einsum('plf,ef->ple', hidden, down_weight_t, preferred_element_type=j...  8.41 us
  transfers between devices with their start and end apart: 4, of which 3 were waited for; matrix products, arithmetic and copies ran while one was open for 34% of the time, Pallas kernels for 0%

profile of v1, /device:TPU:25, one launch (start us, length us, event | category | flops | bytes accessed | tf_op | source)
XLA Modules:
  0.0 245.6 jit_solution(7026375357009473060)
XLA Ops:
  7.2 0.0 copy-start.4
  7.2 0.0 all-gather.2.cloned.1.call-start
  7.2 0.9 convert_bitcast_fusion.1
  8.1 0.9 convert_element_type.45
  9.0 0.8 convert_bitcast_fusion.3
  9.8 0.9 copy_bitcast_fusion
  10.7 0.1 broadcast_in_dim.36
  10.8 0.1 pad_maximum_fusion
  10.9 22.5 %all_to_all.30 = bf16[8,8,9600]{2,0,1:T(8,128)(2,1)S(1)} all-to-all(bf16[8,8,9600]{2,0,1:T(8,128)(2,1)S(1)} %pad_maximum_fusion), channel_id=1, replica_groups=mesh['seq'=16,'head'=8] {'head'}, dimensions={1} | all-to-all | bytes 2457600 | tf_op jit(solution)/shard_map/all_to_all | solution.py:35
  33.4 0.0 copy-start
  33.4 0.9 slice.52
  34.3 0.0 all-gather.2.cloned.1.call-update
  34.3 1.0 broadcast_in_dim.37
  35.3 8.3 %all-to-all-start.1 = ((bf16[16,64,384]{2,1,0:T(8,128)(2,1)}), bf16[16,64,384]{2,1,0:T(8,128)(2,1)S(1)}, u32[]{:S(2)}, u32[]{:S(2)}) async-start(bf16[16,64,384]{2,1,0:T(8,128)(2,1)} %broadcast_in_dim.37), calls=%async_computation.1 | async-start | bytes 1572864 | tf_op jit(solution)/shard_map/all_to_all | solution.py:39
  43.6 0.0 copy-done.4
  43.6 0.1 iota_compare_fusion
  43.7 16.5 %all-to-all-done.1 = bf16[16,64,384]{2,1,0:T(8,128)(2,1)S(1)} async-done(((bf16[16,64,384]{2,1,0:T(8,128)(2,1)}), bf16[16,64,384]{2,1,0:T(8,128)(2,1)S(1)}, u32[]{:S(2)}, u32[]{:S(2)}) %all-to-all-start.1) | async-done | bytes 786464 | tf_op jit(solution)/shard_map/all_to_all | solution.py:39
  60.2 1.1 reshape.101
  61.3 0.0 copy-done
  61.3 7.4 %convert_bitcast_fusion = bf16[8,512,3,128]{1,3,0,2:T(8,128)(2,1)S(1)} fusion(bf16[8,512,1024]{2,1,0:T(8,128)(2,1)} %param.8, bf16[1024,3,128,1]{2,1,0,3:T(4,128)(2,1)} %bitcast.71), kind=kOutput, calls=%fused_computation.32 | convolution fusion | flops 3222798336 | bytes 12320768 | tf_op jit(solution)/shard_map/pld,dte->plte/dot_general | solution.py:74
  68.6 1.8 fusion.28
  70.4 10.8 %fusion.31 = (f32[8,2,512]{2,1,0:T(2,128)S(1)}, f32[8,2,512,512]{2,3,1,0:T(8,128)}) fusion(pred[8,512]{1,0:T(8,128)(4,1)S(1)} %iota_compare_fusion, bf16[8,512,2,64]{1,3,2,0:T(8,128)(2,1)} %bitcast.74, bf16[8,512,2,64]{1,3,2,0:T(8,128)(2,1)} %bitcast.73), kind=kOutput, calls=%fused_computation.62 | convolution fusion | flops 553648640 | bytes 18911232 | tf_op jit(solution)/shard_map/sub | solution.py:89
  81.2 9.0 %fusion.24 = bf16[8,512,2,64]{1,3,2,0:T(8,128)(2,1)} fusion(bf16[8,512,2,64]{1,3,2,0:T(8,128)(2,1)} %bitcast.72, f32[8,2,512,512]{2,3,1,0:T(8,128)} %get-tuple-element.22, f32[8,2,512]{2,1,0:T(2,128)S(1)} %get-tuple-element.21), kind=kOutput, calls=%fused_computation.41 | convolution fusion | flops 545783808 | bytes 18907136 | tf_op jit(solution)/shard_map/phqk,pkhd->pqhd/dot_general | solution.py:91
  90.2 3.9 %reshape.102 = bf16[8,8,64,128]{2,1,3,0:T(8,128)(2,1)} reshape(bf16[8,512,2,64]{1,3,2,0:T(8,128)(2,1)} %fusion.24) | data formatting | bytes 2097152 | tf_op jit(solution)/shard_map/reshape | solution.py:94
  94.1 3.4 %copy.28 = bf16[8,8,64,128]{3,2,1,0:T(8,128)(2,1)} copy(bf16[8,8,64,128]{2,0,3,1:T(8,128)(2,1)} %bitcast.66) | data formatting | bytes 2097152 | tf_op jit(solution)/shard_map/transpose | solution.py:97
  97.5 7.9 %all-to-all-start.2 = ((bf16[8,8,64,128]{3,2,1,0:T(8,128)(2,1)}), bf16[8,8,64,128]{3,2,1,0:T(8,128)(2,1)}, u32[]{:S(2)}, u32[]{:S(2)}) async-start(bf16[8,8,64,128]{3,2,1,0:T(8,128)(2,1)} %copy.28), calls=%async_computation.2 | async-start | bytes 2097152 | tf_op jit(solution)/shard_map/all_to_all | solution.py:98
  105.3 1.9 slice.55
  107.2 13.3 %all-to-all-done.2 = bf16[8,8,64,128]{3,2,1,0:T(8,128)(2,1)} async-done(((bf16[8,8,64,128]{3,2,1,0:T(8,128)(2,1)}), bf16[8,8,64,128]{3,2,1,0:T(8,128)(2,1)}, u32[]{:S(2)}, u32[]{:S(2)}) %all-to-all-start.2) | async-done | bytes 1048608 | tf_op jit(solution)/shard_map/all_to_all | solution.py:98
  120.5 5.3 %stack.2 = bf16[16,64,4096]{2,1,0:T(8,128)(2,1)} broadcast(bf16[64,4096]{1,0:T(8,128)(2,1)} %slice.55), dimensions={1,2} | broadcast | bytes 8912896 | tf_op jit(solution)/shard_map/stack | solution.py:47
  125.8 0.0 copy-start.2
  125.8 0.0 copy-start.3
  125.8 7.4 %all-to-all-start.3 = ((bf16[16,64,4096]{2,1,0:T(8,128)(2,1)}), bf16[16,64,4096]{2,1,0:T(8,128)(2,1)}, u32[]{:S(2)}, u32[]{:S(2)}) async-start(bf16[16,64,4096]{2,1,0:T(8,128)(2,1)} %stack.2), calls=%async_computation.3 | async-start | bytes 16777216 | tf_op jit(solution)/shard_map/all_to_all | solution.py:48
  133.2 0.1 constant_dynamic-slice_fusion
  133.3 0.0 copy-done.2
  133.3 0.0 copy-done.3
  133.4 1.5 bitcast_select_fusion
  134.8 2.3 copy.32
  137.1 2.3 copy.33
  139.3 0.0 all-gather.2.cloned.1.call-done
  139.3 1.8 slice.53
  141.1 2.6 %copy.29 = bf16[1024,1024]{0,1:T(8,128)(2,1)} copy(bf16[1024,1024]{1,0:T(8,128)(2,1)S(1)} %slice.53) | data formatting | bytes 4194304 | tf_op jit(solution)/shard_map/slice | solution.py:43
  143.7 0.0 copy-start.1
  143.7 3.7 %fusion.32 = (f32[8,64]{1,0:T(8,128)S(1)}, f32[8,64,1024]{2,1,0:T(8,128)S(1)}) fusion(bf16[8,8,64,128]{3,2,1,0:T(8,128)(2,1)} %all-to-all-done.2, bf16[1024,8,128,1]{0,2,3,1:T(8,128)(2,1)} %bitcast.70, bf16[8,512,1024]{2,1,0:T(8,128)(2,1)} %param.8, s32[]{:T(128)S(6)} %select_n.19), kind=kOutput, calls=%fused_computation.63 | convolution fusion | flops 1075314176 | bytes 6293508 | tf_op jit(solution)/shard_map/sprf,esf->pre/dot_general | solution.py:100
  147.3 0.3 multiply_reduce_fusion.1
  147.7 1.2 copy-done.1
  148.9 23.4 %fusion.4 = bf16[8,64,4096]{2,1,0:T(8,128)(2,1)} fusion(bf16[1024,5120]{1,0:T(8,128)(2,1)S(1)} %copy-done.1, f32[8,64,1024]{2,1,0:T(8,128)S(1)} %get-tuple-element.24, f32[1024]{0:T(1024)S(1)} %bitcast.79, f32[1024]{0:T(1024)S(1)} %bitcast.77, f32[8,64]{1,0:T(8,128)S(1)} %add_rsqrt_fusion.1, f32[8,64]{1,0:T(8,128)S(1)} %broadcast_multiply_fusion.1), kind=kOutput, calls=%fused_computation.8 | convolution fusion | flops 4433903616 | bytes 14696448 | tf_op jit(solution)/shard_map/pld,df->plf/dot_general | solution.py:108
  172.3 55.1 %all-to-all-done.3 = bf16[16,64,4096]{2,1,0:T(8,128)(2,1)} async-done(((bf16[16,64,4096]{2,1,0:T(8,128)(2,1)}), bf16[16,64,4096]{2,1,0:T(8,128)(2,1)}, u32[]{:S(2)}, u32[]{:S(2)}) %all-to-all-start.3) | async-done | bytes 8388640 | tf_op jit(solution)/shard_map/all_to_all | solution.py:48
  227.4 8.4 %fusion.33 = (f32[8,64]{1,0:T(8,128)S(1)}, f32[8,64,1024]{2,1,0:T(8,128)S(1)}) fusion(bf16[8,64,4096]{2,1,0:T(8,128)(2,1)} %fusion.4, bf16[1024,4096,1]{1,0,2:T(8,128)(2,1)} %bitcast.25, f32[1024]{0:T(1024)S(1)} %bitcast.80, f32[1024]{0:T(1024)S(1)} %bitcast.78, f32[8,64]{1,0:T(8,128)S(1)} %add_rsqrt_fusion.1, f32[8,64,1024]{2,1,0:T(8,128)S(1)} %get-tuple-element.24, ...), kind=kOutput, calls=%fused_computation.64 | convolution fusion | flops 4299161088 | bytes 16791552 | tf_op jit(solution)/shard_map/plf,ef->ple/dot_general | solution.py:112
  235.8 0.3 multiply_reduce_fusion
  236.2 2.6 %select_convert_fusion = bf16[8,64,1024]{2,1,0:T(8,128)(2,1)} fusion(f32[8,64,1024]{2,1,0:T(8,128)S(1)} %get-tuple-element.26, f32[1024]{0:T(1024)S(1)} %bitcast.76, f32[1024]{0:T(1024)S(1)} %bitcast.75, f32[8,64]{1,0:T(8,128)S(1)} %add_rsqrt_fusion, f32[8,64]{1,0:T(8,128)S(1)} %broadcast_multiply_fusion, pred[8,64]{1,0:T(8,128)(4,1)S(1)} %constant_dynamic-slice_fusion), kind=kLoop, calls=%fused_computation.34 | loop fusion | flops 3145728 | bytes 3158528 | tf_op jit(solution)/shard_map/convert_element_type | solution.py:115
  (8 shorter events, 0.1 us)
Async XLA Ops:
  7.2 36.5 %copy-start.4 = (s32[8]{0:T(128)S(1)}, s32[8]{0:T(128)}, u32[]{:S(2)}) copy-start(s32[8]{0:T(128)} %param.9) | copy-start | bytes 100
  7.2 132.2 %all-gather.2.cloned.1.call-start = ((), (), s32[]{:S(2)}) async-start(), calls=%async_computation.4 | async-start | bytes 11141120 | tf_op jit(solution)/shard_map/all_gather | solution.py:42
  33.4 27.9 %copy-start = (bf16[8,8,9600]{2,0,1:T(8,128)(2,1)}, bf16[8,8,9600]{2,0,1:T(8,128)(2,1)S(1)}, u32[]{:S(2)}) copy-start(bf16[8,8,9600]{2,0,1:T(8,128)(2,1)S(1)} %all_to_all.30) | copy-start | bytes 3686404
  35.3 24.9 %all-to-all-start.1 = ((bf16[16,64,384]{2,1,0:T(8,128)(2,1)}), bf16[16,64,384]{2,1,0:T(8,128)(2,1)S(1)}, u32[]{:S(2)}, u32[]{:S(2)}) async-start(bf16[16,64,384]{2,1,0:T(8,128)(2,1)} %broadcast_in_dim.37), calls=%async_computation.1 | async-start | bytes 1572864 | tf_op jit(solution)/shard_map/all_to_all | solution.py:39
  97.5 23.0 %all-to-all-start.2 = ((bf16[8,8,64,128]{3,2,1,0:T(8,128)(2,1)}), bf16[8,8,64,128]{3,2,1,0:T(8,128)(2,1)}, u32[]{:S(2)}, u32[]{:S(2)}) async-start(bf16[8,8,64,128]{3,2,1,0:T(8,128)(2,1)} %copy.28), calls=%async_computation.2 | async-start | bytes 2097152 | tf_op jit(solution)/shard_map/all_to_all | solution.py:98
  125.8 7.5 %copy-start.2 = (f32[2,1024]{1,0:T(2,128)S(1)}, f32[2,1024]{1,0:T(2,128)}, u32[]{:S(2)}) copy-start(f32[2,1024]{1,0:T(2,128)} %param.14) | copy-start | bytes 24580
  125.8 7.5 %copy-start.3 = (f32[2,1024]{1,0:T(2,128)S(1)}, f32[2,1024]{1,0:T(2,128)}, u32[]{:S(2)}) copy-start(f32[2,1024]{1,0:T(2,128)} %param.15) | copy-start | bytes 24580
  125.8 101.6 %all-to-all-start.3 = ((bf16[16,64,4096]{2,1,0:T(8,128)(2,1)}), bf16[16,64,4096]{2,1,0:T(8,128)(2,1)}, u32[]{:S(2)}, u32[]{:S(2)}) async-start(bf16[16,64,4096]{2,1,0:T(8,128)(2,1)} %stack.2), calls=%async_computation.3 | async-start | bytes 16777216 | tf_op jit(solution)/shard_map/all_to_all | solution.py:48
  143.7 5.2 %copy-start.1 = (bf16[1024,5120]{1,0:T(8,128)(2,1)S(1)}, bf16[1024,5120]{1,0:T(8,128)(2,1)}, u32[]{:S(2)}) copy-start(bf16[1024,5120]{1,0:T(8,128)(2,1)} %all-gather.2.cloned.1.call-done) | copy-start | bytes 31457284
Sparse Core Ops, SparseCore 0:
  34.4 71.1 all-gather.1
